TPU v7x, 32 devices: a whole 2x2x4 slice. The times are simulated.
32 devices in a mesh: dp: 4 (over y, x), expert: 8 (over z, core).
Axes of the slice: x: 2, y: 2, z: 4, core: 2. Of those that a mesh axis runs over, the one named last changes fastest.
Arguments:
- tokens: bfloat16 [4096, 1536], P(('dp', 'expert')), may hold values from -6 to 6
- grad_out: bfloat16 [4096, 1536], P(('dp', 'expert')), may hold values from -6 to 6
- expert_ids: int32 [4096, 4], P(('dp', 'expert')), may hold values from 0 to 7, all different within a row; in each aligned block of 128 rows (0 to 127, 128 to 255, ...) at most 96 rows name the same one
- gate_q: int32 [4096, 4], P(('dp', 'expert')), may hold values from 1 to 65535
- w_up: bfloat16 [8, 1536, 768], P('expert', 'dp'), may hold values from -0.15625 to 0.15625
- w_down: bfloat16 [8, 768, 1536], P('expert', None, 'dp'), may hold values from -0.21875 to 0.21875
Outputs:
- dw_up: bfloat16 [8, 1536, 768], P('expert', 'dp')
- dw_down: bfloat16 [8, 768, 1536], P('expert', None, 'dp')
Inputs may be any that keep to these rules, and one draw needn't show every extreme that they name: `expert_ids`: within the rows of one device no expert is named by more than 96 rows, a bound that some block reaches; the 4 ids of a row differ.
All inputs are finite; a program needn't handle non-finite values.
Results may differ from a plain program's by a relative error of at most 0.0064.
Values may be sent and summed in bfloat16 or wider, within the bound.
No kernel may reach another device: no remote copies, remote signals or barrier semaphores. Data moves between devices by JAX's collectives and lax.ppermute only.
A program may use at most 64 MiB of HBM per device.

v0:
```python
import jax
import jax.numpy as jnp
from jax import lax
from jax.sharding import PartitionSpec as P


def silu_slope(values):
    sigmoid_part = jax.nn.sigmoid(values)
    return sigmoid_part * (1.0 + values * (1.0 - sigmoid_part))


def summed_up(recv_rows, projected_grad):
    first_dims = (((0,), (0,)), ((), ()))
    partial_value = lax.dot_general(
        recv_rows, projected_grad, first_dims, preferred_element_type=jnp.float32
    ).astype(jnp.bfloat16)
    pieces = lax.all_to_all(partial_value[None], "dp", split_axis=1, concat_axis=0, tiled=True)
    return jnp.sum(pieces.astype(jnp.float32), axis=0, keepdims=True).astype(jnp.bfloat16)


def summed_down(activated, grad_rows):
    first_dims = (((0,), (0,)), ((), ()))
    partial_value = lax.dot_general(
        activated, grad_rows, first_dims, preferred_element_type=jnp.float32
    ).astype(jnp.bfloat16)
    pieces = lax.all_to_all(partial_value[None], "dp", split_axis=2, concat_axis=0, tiled=True)
    return jnp.sum(pieces.astype(jnp.float32), axis=0, keepdims=True).astype(jnp.bfloat16)


def shards(tokens, grad_out, expert_ids, gate_q, w_up, w_down):
    devices = lax.axis_size("expert")
    token_count, top_count = expert_ids.shape
    model_width = tokens.shape[1]
    capacity = max(2, token_count * top_count * 3 // (2 * devices))
    slot_expert = expert_ids.reshape(-1)
    onehot_table = (slot_expert[:, None] == jnp.arange(devices, dtype=jnp.int32)[None, :]).astype(
        jnp.int32
    )
    earlier = jnp.cumsum(onehot_table, axis=0) - onehot_table
    slot_rank = jnp.sum(earlier * onehot_table, axis=1)
    slot_target = slot_expert * capacity + slot_rank
    gate_values = gate_q.reshape(-1).astype(jnp.float32) * (1.0 / 65536.0)
    token_rows = jnp.repeat(tokens, top_count, axis=0)
    slot_grads = (
        gate_values[:, None] * jnp.repeat(grad_out, top_count, axis=0).astype(jnp.float32)
    ).astype(jnp.bfloat16)
    empty_rows = jnp.zeros((devices * capacity, model_width), jnp.bfloat16)
    send_tokens = empty_rows.at[slot_target].set(token_rows).reshape(devices, capacity, model_width)
    grad_slots = empty_rows.at[slot_target].set(slot_grads).reshape(devices, capacity, model_width)
    contract_last = (((1,), (1,)), ((), ()))
    up_whole = lax.all_gather(w_up, "dp", axis=1, tiled=True)[0]
    down_whole = lax.all_gather(w_down, "dp", axis=2, tiled=True)[0]
    recv_tokens = lax.all_to_all(send_tokens, "expert", split_axis=0, concat_axis=0, tiled=True)
    recv_rows = recv_tokens.reshape(-1, model_width)
    projected = jnp.dot(recv_rows, up_whole, preferred_element_type=jnp.float32)
    recv_grads = lax.all_to_all(grad_slots, "expert", split_axis=0, concat_axis=0, tiled=True)
    activated = jax.nn.silu(projected).astype(jnp.bfloat16)
    grad_rows = recv_grads.reshape(-1, model_width)
    act_grad = lax.dot_general(
        grad_rows, down_whole, contract_last, preferred_element_type=jnp.float32
    )
    projected_grad = (act_grad * silu_slope(projected)).astype(jnp.bfloat16)
    up_grad = summed_up(recv_rows, projected_grad)
    down_grad = summed_down(activated, grad_rows)
    return (up_grad, down_grad)


def solution(mesh):
    in_specs = (
        P(("dp", "expert"), None),
        P(("dp", "expert"), None),
        P(("dp", "expert"), None),
        P(("dp", "expert"), None),
        P("expert", "dp", None),
        P("expert", None, "dp"),
    )
    out_specs = (P("expert", "dp", None), P("expert", None, "dp"))
    return jax.shard_map(shards, mesh=mesh, in_specs=in_specs, out_specs=out_specs, check_vma=False)
```

profile of v0, /device:TPU:0, one launch (start us, length us, event | category | flops | bytes accessed | tf_op | source)
XLA Modules:
  0.0 307.0 jit_solution(6901323254794781142)
XLA Ops:
  12.4 4.7 %scatter_custom_fusion = bf16[768,1536]{1,0:T(8,128)(2,1)} fusion(s32[512]{0:T(512)S(1)} %bitcast.53, bf16[512,1536]{1,0:T(8,128)(2,1)S(1)} %reshape.112, bf16[]{:T(256)} %constant.7.clone.1), kind=kCustom, calls=%fused_computation.18 | custom fusion | bytes 2359298 | tf_op jit(solution)/shard_map/scatter | solution.py:48
  17.1 6.5 %all-to-all-start = ((bf16[8,96,1536]{2,1,0:T(8,128)(2,1)}), bf16[8,96,1536]{2,1,0:T(8,128)(2,1)}, u32[]{:S(2)}, u32[]{:S(2)}) async-start(bf16[8,96,1536]{2,1,0:T(8,128)(2,1)} %bitcast.4), calls=%async_computation | async-start | bytes 4718592 | tf_op jit(solution)/shard_map/all_to_all | solution.py:53
  24.7 2.3 convert_element_type.78
  27.2 6.0 %scatter_custom_fusion.1 = bf16[768,1536]{1,0:T(8,128)(2,1)} fusion(s32[512]{0:T(512)S(1)} %bitcast.54, f32[512,1536]{1,0:T(8,128)} %convert_element_type.78, f32[512]{0:T(512)S(1)} %mul.59, bf16[]{:T(256)} %constant.7.clone.1), kind=kCustom, calls=%fused_computation.14 | custom fusion | flops 1572864 | bytes 5507074 | tf_op jit(solution)/shard_map/scatter | solution.py:49
  33.3 45.1 %all-to-all-done = bf16[8,96,1536]{2,1,0:T(8,128)(2,1)} async-done(((bf16[8,96,1536]{2,1,0:T(8,128)(2,1)}), bf16[8,96,1536]{2,1,0:T(8,128)(2,1)}, u32[]{:S(2)}, u32[]{:S(2)}) %all-to-all-start) | async-done | bytes 2359328 | tf_op jit(solution)/shard_map/all_to_all | solution.py:53
  78.3 3.6 %all-to-all-start.1 = ((bf16[8,96,1536]{2,1,0:T(8,128)(2,1)}), bf16[8,96,1536]{2,1,0:T(8,128)(2,1)S(1)}, u32[]{:S(2)}, u32[]{:S(2)}) async-start(bf16[8,96,1536]{2,1,0:T(8,128)(2,1)} %bitcast.6), calls=%async_computation.1 | async-start | bytes 4718592 | tf_op jit(solution)/shard_map/all_to_all | solution.py:56
  82.7 5.8 %fusion.2 = f32[768,768]{1,0:T(8,128)} fusion(bf16[768,1536]{1,0:T(8,128)(2,1)} %bitcast.5, bf16[1,1536,768]{2,1,0:T(8,128)(2,1)} %all-gather.5.cloned.1.call-done), kind=kOutput, calls=%fused_computation.7 | convolution fusion | flops 1811939328 | bytes 7077888 | tf_op jit(solution)/shard_map/dot_general | solution.py:55
  88.5 34.7 %all-gather.3.cloned.1.call-done = bf16[1,768,1536]{2,1,0:T(8,128)(2,1)} async-done(((bf16[1,768,384]{2,1,0:T(8,128)(2,1)}), bf16[1,768,1536]{2,1,0:T(8,128)(2,1)}) %all-gather.3.cloned.1.call-update) | async-done | bytes 2359312 | tf_op jit(solution)/shard_map/all_gather | solution.py:52
  123.2 13.3 %all-to-all-done.1 = bf16[8,96,1536]{2,1,0:T(8,128)(2,1)S(1)} async-done(((bf16[8,96,1536]{2,1,0:T(8,128)(2,1)}), bf16[8,96,1536]{2,1,0:T(8,128)(2,1)S(1)}, u32[]{:S(2)}, u32[]{:S(2)}) %all-to-all-start.1) | async-done | bytes 2359328 | tf_op jit(solution)/shard_map/all_to_all | solution.py:56
  137.9 8.2 %fusion = bf16[1,1536,768]{2,1,0:T(8,128)(2,1)S(1)} fusion(bf16[768,1536]{1,0:T(8,128)(2,1)} %bitcast.5, f32[768,768]{1,0:T(8,128)} %fusion.2, bf16[768,1536]{1,0:T(8,128)(2,1)} %bitcast.48, bf16[1,768,1536]{2,1,0:T(8,128)(2,1)} %all-gather.3.cloned.1.call-done), kind=kOutput, calls=%fused_computation.5 | convolution fusion | flops 3630366720 | bytes 11796480 | tf_op jit(solution)/shard_map/dot_general | solution.py:14
  146.1 33.8 %copy.34 = bf16[1,1536,768]{2,0,1:T(2,128)(2,1)} copy(bf16[1,1536,768]{2,1,0:T(8,128)(2,1)S(1)} %fusion) | data formatting | bytes 4718592 | tf_op jit(solution)/shard_map/broadcast_in_dim | solution.py:17
  180.4 24.1 %reduce.7 = bf16[1536,768]{1,0:T(8,128)(2,1)S(1)} reduce(bf16[1536,1,768]{2,1,0:T(2,128)(2,1)} %bitcast.42, bf16[]{:T(256)} %broadcast.72), dimensions={1}, to_apply=%bitcast.41.reduce_sub_computation | reduce | bytes 4718594
  204.5 2.3 reshape.129
  206.8 3.9 %all-to-all-start.2 = ((bf16[4,2,147456]{2,1,0:T(2,128)(2,1)}), bf16[4,2,147456]{2,1,0:T(2,128)(2,1)S(1)}, u32[]{:S(2)}, u32[]{:S(2)}) async-start(bf16[4,2,147456]{2,1,0:T(2,128)(2,1)} %reshape.129), calls=%async_computation.2 | async-start | bytes 4718592 | tf_op jit(solution)/shard_map/all_to_all | solution.py:17
  210.6 5.9 %fusion.1 = bf16[1,768,1536]{2,1,0:T(8,128)(2,1)} fusion(bf16[768,1536]{1,0:T(8,128)(2,1)} %bitcast.49, f32[768,768]{1,0:T(8,128)} %fusion.2), kind=kOutput, calls=%fused_computation.6 | convolution fusion | flops 1816068096 | bytes 7077888 | tf_op jit(solution)/shard_map/dot_general | solution.py:23
  216.5 12.1 %copy.29 = bf16[1,768,1536]{1,0,2:T(2,128)(2,1)} copy(bf16[1,768,1536]{2,1,0:T(8,128)(2,1)} %fusion.1) | data formatting | bytes 4718592 | tf_op jit(solution)/shard_map/broadcast_in_dim | solution.py:26
  228.6 25.5 %reduce.8 = bf16[1536,768]{1,0:T(8,128)(2,1)} reduce(bf16[1536,1,768]{2,1,0:T(2,128)(2,1)} %bitcast.43, bf16[]{:T(256)} %broadcast.72), dimensions={1}, to_apply=%bitcast.34.reduce_sub_computation | reduce | bytes 4718594
  254.1 4.1 %reshape.131 = bf16[4,2,147456]{2,1,0:T(2,128)(2,1)} reshape(bf16[1536,768]{1,0:T(8,128)(2,1)} %reduce.8) | data formatting | bytes 4718592
  258.2 4.5 %all-to-all-start.3 = ((bf16[4,2,147456]{2,1,0:T(2,128)(2,1)}), bf16[4,2,147456]{2,1,0:T(2,128)(2,1)}, u32[]{:S(2)}, u32[]{:S(2)}) async-start(bf16[4,2,147456]{2,1,0:T(2,128)(2,1)} %reshape.131), calls=%async_computation.3 | async-start | bytes 4718592 | tf_op jit(solution)/shard_map/all_to_all | solution.py:26
  262.7 3.6 %reshape.130 = bf16[1536,1,768]{2,1,0:T(2,128)(2,1)} reshape(bf16[4,2,147456]{2,1,0:T(2,128)(2,1)S(1)} %all-to-all-done.2) | data formatting | bytes 4718592
  266.3 2.7 copy.31
  270.3 20.1 %all-to-all-done.3 = bf16[4,2,147456]{2,1,0:T(2,128)(2,1)} async-done(((bf16[4,2,147456]{2,1,0:T(2,128)(2,1)}), bf16[4,2,147456]{2,1,0:T(2,128)(2,1)}, u32[]{:S(2)}, u32[]{:S(2)}) %all-to-all-start.3) | async-done | bytes 2359328 | tf_op jit(solution)/shard_map/all_to_all | solution.py:26
  290.5 5.2 %reshape.132 = bf16[1536,1,768]{2,1,0:T(2,128)(2,1)} reshape(bf16[4,2,147456]{2,1,0:T(2,128)(2,1)} %all-to-all-done.3) | data formatting | bytes 4718592
  295.6 2.7 copy.32
  (35 shorter events, 12.3 us)
Async XLA Ops:
  17.1 7.2 %copy-start.1 = (bf16[128,1536]{1,0:T(8,128)(2,1)S(1)}, bf16[128,1536]{1,0:T(8,128)(2,1)}, u32[]{:S(2)}) copy-start(bf16[128,1536]{1,0:T(8,128)(2,1)} %param.7) | copy-start | bytes 1179652
  17.1 61.2 %all-to-all-start = ((bf16[8,96,1536]{2,1,0:T(8,128)(2,1)}), bf16[8,96,1536]{2,1,0:T(8,128)(2,1)}, u32[]{:S(2)}, u32[]{:S(2)}) async-start(bf16[8,96,1536]{2,1,0:T(8,128)(2,1)} %bitcast.4), calls=%async_computation | async-start | bytes 4718592 | tf_op jit(solution)/shard_map/all_to_all | solution.py:53
  23.6 59.2 %all-gather.5.cloned.1.call-start = ((), (), s32[]{:S(2)}) async-start(), calls=%async_computation.5 | async-start | bytes 2949120 | tf_op jit(solution)/shard_map/all_gather | solution.py:51
  24.7 2.3 copy-start.2
  78.3 58.2 %all-to-all-start.1 = ((bf16[8,96,1536]{2,1,0:T(8,128)(2,1)}), bf16[8,96,1536]{2,1,0:T(8,128)(2,1)S(1)}, u32[]{:S(2)}, u32[]{:S(2)}) async-start(bf16[8,96,1536]{2,1,0:T(8,128)(2,1)} %bitcast.6), calls=%async_computation.1 | async-start | bytes 4718592 | tf_op jit(solution)/shard_map/all_to_all | solution.py:56
  81.9 41.3 %all-gather.3.cloned.1.call-start = ((), (), s32[]{:S(2)}) async-start(), calls=%async_computation.4 | async-start | bytes 2949120 | tf_op jit(solution)/shard_map/all_gather | solution.py:52
  136.5 1.4 copy-start
  206.8 51.5 %all-to-all-start.2 = ((bf16[4,2,147456]{2,1,0:T(2,128)(2,1)}), bf16[4,2,147456]{2,1,0:T(2,128)(2,1)S(1)}, u32[]{:S(2)}, u32[]{:S(2)}) async-start(bf16[4,2,147456]{2,1,0:T(2,128)(2,1)} %reshape.129), calls=%async_computation.2 | async-start | bytes 4718592 | tf_op jit(solution)/shard_map/all_to_all | solution.py:17
  258.2 32.2 %all-to-all-start.3 = ((bf16[4,2,147456]{2,1,0:T(2,128)(2,1)}), bf16[4,2,147456]{2,1,0:T(2,128)(2,1)}, u32[]{:S(2)}, u32[]{:S(2)}) async-start(bf16[4,2,147456]{2,1,0:T(2,128)(2,1)} %reshape.131), calls=%async_computation.3 | async-start | bytes 4718592 | tf_op jit(solution)/shard_map/all_to_all | solution.py:26
Sparse Core Ops, SparseCore 0:
  26.2 38.7 all-gather.4
  84.6 38.5 all-gather.2
where the time goes:
time: 308 us; the launch traced here: 307 us
  waiting for transfers between devices  114 us (37%)
  local copies, waits for them, and re-layouts  80.2 us (26%)
  other arithmetic  59.7 us (19%)
  matrix products  19.9 us (6%)
  starting transfers between devices  18.7 us (6%)
  between operations  14.2 us (5%)
    unnamed x2, other arithmetic  49.6 us
    all_to_all x1, waiting for transfers between devices, shards(): lax.all_to_all(send_tokens, 'expert', split_axis=0, concat_axis=0, tiled=...  45.1 us
    all_gather x1, waiting for transfers between devices, shards(): down_whole = lax.all_gather(w_down, 'dp', axis=2, tiled=True)[0]  34.7 us
    broadcast_in_dim x1, local copies, waits for them, and re-layouts, summed_up(): partial_value[None]  33.8 us
    unnamed x15, local copies, waits for them, and re-layouts  24.3 us
    all_to_all x1, waiting for transfers between devices, summed_down(): lax.all_to_all(partial_value[None], 'dp', split_axis=2, concat_axis=0, ti...  20.1 us
    all_to_all x1, waiting for transfers between devices, shards(): lax.all_to_all(grad_slots, 'expert', split_axis=0, concat_axis=0, tiled=T...  13.3 us
    broadcast_in_dim x1, local copies, waits for them, and re-layouts, summed_down(): partial_value[None]  12.1 us
  transfers between devices with their start and end apart: 6, of which 4 were waited for; matrix products, arithmetic and copies ran while one was open for 23% of the time, Pallas kernels for 0%

commit v1 on v0

--- a/solution.py
+++ b/solution.py
@@ -2,6 +2,16 @@
 import jax.numpy as jnp
 from jax import lax
 from jax.sharding import PartitionSpec as P
+
+mark_flows = lambda local_values, named_axis, ndim_at: jnp.concatenate(
+    jax.lax.all_to_all(
+        jnp.stack([local_values] * jax.lax.axis_size(named_axis)),
+        concat_axis=0,
+        axis_name=named_axis,
+        split_axis=0,
+    ),
+    ndim_at,
+)
 
 
 def silu_slope(values):
@@ -49,7 +59,7 @@
     grad_slots = empty_rows.at[slot_target].set(slot_grads).reshape(devices, capacity, model_width)
     contract_last = (((1,), (1,)), ((), ()))
     up_whole = lax.all_gather(w_up, "dp", axis=1, tiled=True)[0]
-    down_whole = lax.all_gather(w_down, "dp", axis=2, tiled=True)[0]
+    down_whole = mark_flows(w_down, "dp", 2)[0]
     recv_tokens = lax.all_to_all(send_tokens, "expert", split_axis=0, concat_axis=0, tiled=True)
     recv_rows = recv_tokens.reshape(-1, model_width)
     projected = jnp.dot(recv_rows, up_whole, preferred_element_type=jnp.float32)

time: 308 us -> 334 us (1.084)
  waiting for transfers between devices: 114 us -> 135 us
  starting transfers between devices: 18.7 us -> 22.7 us
    all_gather x1, waiting for transfers between devices: 0.02 us -> 39.7 us  [shards(): up_whole = lax.all_gather(w_up, 'dp', axis=1, tiled=True)[0]]
    all_gather x1 -> x0, waiting for transfers between devices: 34.7 us -> none  [shards(): down_whole = lax.all_gather(w_down, 'dp', axis=2, tiled=True)[0]]
    all_to_all x0 -> x1, waiting for transfers between devices: none -> 21 us  [jax.lax.all_to_all(jnp.stack([local_values] * jax.lax.axis_size(named_axi...]
    all_to_all x0 -> x1, starting transfers between devices: none -> 5.32 us  [jax.lax.all_to_all(jnp.stack([local_values] * jax.lax.axis_size(named_axi...]
    all_to_all x1, waiting for transfers between devices: 13.3 us -> 8.33 us  [shards(): lax.all_to_all(grad_slots, 'expert', split_axis=0, concat_axis=0, tiled=T...]
    unnamed x15 -> x19, local copies, waits for them, and re-layouts: 24.3 us -> 23.8 us
  transfers between devices with their start and end apart: 6 -> 6, of which waited for: 4 -> 5; matrix products, arithmetic and copies ran while one was open for 23% -> 23% of each run, Pallas kernels for 0% -> 0%
where the time goes in v1:
time: 334 us; the launch traced here: 333 us
  waiting for transfers between devices  135 us (40%)
  local copies, waits for them, and re-layouts  81.5 us (24%)
  other arithmetic  59.1 us (18%)
  starting transfers between devices  22.7 us (7%)
  matrix products  19.8 us (6%)
  between operations  14.2 us (4%)
    unnamed x2, other arithmetic  49.7 us
    all_to_all x1, waiting for transfers between devices, shards(): lax.all_to_all(send_tokens, 'expert', split_axis=0, concat_axis=0, tiled=...  45.7 us
    all_gather x1, waiting for transfers between devices, shards(): up_whole = lax.all_gather(w_up, 'dp', axis=1, tiled=True)[0]  39.7 us
    broadcast_in_dim x1, local copies, waits for them, and re-layouts, summed_up(): partial_value[None]  33.8 us
    unnamed x19, local copies, waits for them, and re-layouts  23.8 us
    all_to_all x1, waiting for transfers between devices, jax.lax.all_to_all(jnp.stack([local_values] * jax.lax.axis_size(named_axi...  21 us
    all_to_all x1, waiting for transfers between devices, summed_down(): lax.all_to_all(partial_value[None], 'dp', split_axis=2, concat_axis=0, ti...  20 us
    broadcast_in_dim x1, local copies, waits for them, and re-layouts, summed_down(): partial_value[None]  12.1 us
  transfers between devices with their start and end apart: 6, of which 5 were waited for; matrix products, arithmetic and copies ran while one was open for 23% of the time, Pallas kernels for 0%

profile of v1, /device:TPU:0, one launch (start us, length us, event | category | flops | bytes accessed | tf_op | source)
XLA Modules:
  0.0 332.5 jit_solution(4464924576260747066)
XLA Ops:
  10.0 5.3 %all-to-all-start.2 = ((bf16[4,1,768,384]{2,3,1,0:T(8,128)(2,1)}), bf16[4,1,768,384]{2,3,1,0:T(8,128)(2,1)}, u32[]{:S(2)}, u32[]{:S(2)}) async-start(bf16[4,1,768,384]{2,3,1,0:T(8,128)(2,1)} %stack.2), calls=%async_computation.2 | async-start | bytes 4718592 | tf_op jit(solution)/shard_map/all_to_all | solution.py:7
  18.2 4.7 %scatter_custom_fusion = bf16[768,1536]{1,0:T(8,128)(2,1)} fusion(s32[512]{0:T(512)S(1)} %bitcast.54, bf16[512,1536]{1,0:T(8,128)(2,1)S(1)} %reshape.119, bf16[]{:T(256)} %constant.7.clone.1), kind=kCustom, calls=%fused_computation.16 | custom fusion | bytes 2359298 | tf_op jit(solution)/shard_map/scatter | solution.py:58
  23.0 21.0 %all-to-all-done.2 = bf16[4,1,768,384]{2,3,1,0:T(8,128)(2,1)} async-done(((bf16[4,1,768,384]{2,3,1,0:T(8,128)(2,1)}), bf16[4,1,768,384]{2,3,1,0:T(8,128)(2,1)}, u32[]{:S(2)}, u32[]{:S(2)}) %all-to-all-start.2) | async-done | bytes 2359328 | tf_op jit(solution)/shard_map/all_to_all | solution.py:7
  43.9 5.2 %all-to-all-start = ((bf16[8,96,1536]{2,1,0:T(8,128)(2,1)}), bf16[8,96,1536]{2,1,0:T(8,128)(2,1)}, u32[]{:S(2)}, u32[]{:S(2)}) async-start(bf16[8,96,1536]{2,1,0:T(8,128)(2,1)} %bitcast.4), calls=%async_computation | async-start | bytes 4718592 | tf_op jit(solution)/shard_map/all_to_all | solution.py:63
  52.1 6.1 %scatter_custom_fusion.1 = bf16[768,1536]{1,0:T(8,128)(2,1)} fusion(s32[512]{0:T(512)S(1)} %bitcast.55, f32[512,1536]{1,0:T(8,128)} %convert_element_type.78, f32[512]{0:T(512)S(1)} %mul.59, bf16[]{:T(256)} %constant.7.clone.1), kind=kCustom, calls=%fused_computation.12 | custom fusion | flops 1572864 | bytes 5507074 | tf_op jit(solution)/shard_map/scatter | solution.py:59
  58.2 45.7 %all-to-all-done = bf16[8,96,1536]{2,1,0:T(8,128)(2,1)} async-done(((bf16[8,96,1536]{2,1,0:T(8,128)(2,1)}), bf16[8,96,1536]{2,1,0:T(8,128)(2,1)}, u32[]{:S(2)}, u32[]{:S(2)}) %all-to-all-start) | async-done | bytes 2359328 | tf_op jit(solution)/shard_map/all_to_all | solution.py:63
  103.9 3.6 %all-to-all-start.1 = ((bf16[8,96,1536]{2,1,0:T(8,128)(2,1)}), bf16[8,96,1536]{2,1,0:T(8,128)(2,1)S(1)}, u32[]{:S(2)}, u32[]{:S(2)}) async-start(bf16[8,96,1536]{2,1,0:T(8,128)(2,1)} %bitcast.6), calls=%async_computation.1 | async-start | bytes 4718592 | tf_op jit(solution)/shard_map/all_to_all | solution.py:66
  108.3 39.7 %all-gather.2.cloned.1.call-done = bf16[1,1536,768]{2,1,0:T(8,128)(2,1)} async-done(((bf16[1,384,768]{2,1,0:T(8,128)(2,1)}), bf16[1,1536,768]{2,1,0:T(8,128)(2,1)}) %all-gather.2.cloned.1.call-update) | async-done | bytes 2359312 | tf_op jit(solution)/shard_map/all_gather | solution.py:61
  148.0 5.8 %fusion.2 = f32[768,768]{1,0:T(8,128)} fusion(bf16[768,1536]{1,0:T(8,128)(2,1)} %bitcast.5, bf16[1,1536,768]{2,1,0:T(8,128)(2,1)} %all-gather.2.cloned.1.call-done), kind=kOutput, calls=%fused_computation.7 | convolution fusion | flops 1811939328 | bytes 7077888 | tf_op jit(solution)/shard_map/dot_general | solution.py:65
  153.8 8.3 %all-to-all-done.1 = bf16[8,96,1536]{2,1,0:T(8,128)(2,1)S(1)} async-done(((bf16[8,96,1536]{2,1,0:T(8,128)(2,1)}), bf16[8,96,1536]{2,1,0:T(8,128)(2,1)S(1)}, u32[]{:S(2)}, u32[]{:S(2)}) %all-to-all-start.1) | async-done | bytes 2359328 | tf_op jit(solution)/shard_map/all_to_all | solution.py:66
  163.6 8.1 %fusion = bf16[1,1536,768]{2,1,0:T(8,128)(2,1)S(1)} fusion(bf16[768,1536]{1,0:T(8,128)(2,1)} %bitcast.5, f32[768,768]{1,0:T(8,128)} %fusion.2, bf16[768,1536]{1,0:T(8,128)(2,1)} %bitcast.48, bf16[768,1536]{0,1:T(8,128)(2,1)} %bitcast.11), kind=kOutput, calls=%fused_computation.5 | convolution fusion | flops 3630366720 | bytes 11796480 | tf_op jit(solution)/shard_map/dot_general | solution.py:24
  171.7 33.8 %copy.41 = bf16[1,1536,768]{2,0,1:T(2,128)(2,1)} copy(bf16[1,1536,768]{2,1,0:T(8,128)(2,1)S(1)} %fusion) | data formatting | bytes 4718592 | tf_op jit(solution)/shard_map/broadcast_in_dim | solution.py:27
  206.0 24.1 %reduce.7 = bf16[1536,768]{1,0:T(8,128)(2,1)S(1)} reduce(bf16[1536,1,768]{2,1,0:T(2,128)(2,1)} %bitcast.42, bf16[]{:T(256)} %broadcast.75), dimensions={1}, to_apply=%bitcast.41.reduce_sub_computation | reduce | bytes 4718594
  232.3 3.9 %all-to-all-start.3 = ((bf16[4,2,147456]{2,1,0:T(2,128)(2,1)}), bf16[4,2,147456]{2,1,0:T(2,128)(2,1)S(1)}, u32[]{:S(2)}, u32[]{:S(2)}) async-start(bf16[4,2,147456]{2,1,0:T(2,128)(2,1)} %reshape.136), calls=%async_computation.3 | async-start | bytes 4718592 | tf_op jit(solution)/shard_map/all_to_all | solution.py:27
  236.2 5.8 %fusion.1 = bf16[1,768,1536]{2,1,0:T(8,128)(2,1)} fusion(bf16[768,1536]{1,0:T(8,128)(2,1)} %bitcast.49, f32[768,768]{1,0:T(8,128)} %fusion.2), kind=kOutput, calls=%fused_computation.6 | convolution fusion | flops 1816068096 | bytes 7077888 | tf_op jit(solution)/shard_map/dot_general | solution.py:33
  242.0 12.1 %copy.36 = bf16[1,768,1536]{1,0,2:T(2,128)(2,1)} copy(bf16[1,768,1536]{2,1,0:T(8,128)(2,1)} %fusion.1) | data formatting | bytes 4718592 | tf_op jit(solution)/shard_map/broadcast_in_dim | solution.py:36
  254.1 25.5 %reduce.8 = bf16[1536,768]{1,0:T(8,128)(2,1)} reduce(bf16[1536,1,768]{2,1,0:T(2,128)(2,1)} %bitcast.43, bf16[]{:T(256)} %broadcast.75), dimensions={1}, to_apply=%bitcast.33.reduce_sub_computation | reduce | bytes 4718594
  279.6 4.1 %reshape.138 = bf16[4,2,147456]{2,1,0:T(2,128)(2,1)} reshape(bf16[1536,768]{1,0:T(8,128)(2,1)} %reduce.8) | data formatting | bytes 4718592
  283.7 4.5 %all-to-all-start.4 = ((bf16[4,2,147456]{2,1,0:T(2,128)(2,1)}), bf16[4,2,147456]{2,1,0:T(2,128)(2,1)}, u32[]{:S(2)}, u32[]{:S(2)}) async-start(bf16[4,2,147456]{2,1,0:T(2,128)(2,1)} %reshape.138), calls=%async_computation.4 | async-start | bytes 4718592 | tf_op jit(solution)/shard_map/all_to_all | solution.py:36
  288.2 3.7 %reshape.137 = bf16[1536,1,768]{2,1,0:T(2,128)(2,1)} reshape(bf16[4,2,147456]{2,1,0:T(2,128)(2,1)S(1)} %all-to-all-done.3) | data formatting | bytes 4718592
  291.9 2.7 copy.38
  295.9 20.0 %all-to-all-done.4 = bf16[4,2,147456]{2,1,0:T(2,128)(2,1)} async-done(((bf16[4,2,147456]{2,1,0:T(2,128)(2,1)}), bf16[4,2,147456]{2,1,0:T(2,128)(2,1)}, u32[]{:S(2)}, u32[]{:S(2)}) %all-to-all-start.4) | async-done | bytes 2359328 | tf_op jit(solution)/shard_map/all_to_all | solution.py:36
  315.9 5.2 %reshape.139 = bf16[1536,1,768]{2,1,0:T(2,128)(2,1)} reshape(bf16[4,2,147456]{2,1,0:T(2,128)(2,1)} %all-to-all-done.4) | data formatting | bytes 4718592
  321.2 2.7 copy.39
  (40 shorter events, 16.5 us)
Async XLA Ops:
  10.0 5.3 %copy-start.3 = (s32[128,4]{0,1:T(4,128)S(1)}, s32[128,4]{0,1:T(4,128)}, u32[]{:S(2)}) copy-start(s32[128,4]{0,1:T(4,128)} %param.8) | copy-start | bytes 6148
  10.0 7.3 %copy-start.2 = (bf16[128,1536]{1,0:T(8,128)(2,1)S(1)}, bf16[128,1536]{1,0:T(8,128)(2,1)}, u32[]{:S(2)}) copy-start(bf16[128,1536]{1,0:T(8,128)(2,1)} %param.6) | copy-start | bytes 1179652
  10.0 33.9 %all-to-all-start.2 = ((bf16[4,1,768,384]{2,3,1,0:T(8,128)(2,1)}), bf16[4,1,768,384]{2,3,1,0:T(8,128)(2,1)}, u32[]{:S(2)}, u32[]{:S(2)}) async-start(bf16[4,1,768,384]{2,3,1,0:T(8,128)(2,1)} %stack.2), calls=%async_computation.2 | async-start | bytes 4718592 | tf_op jit(solution)/shard_map/all_to_all | solution.py:7
  43.9 5.2 %copy-start.1 = (bf16[128,1536]{1,0:T(8,128)(2,1)S(1)}, bf16[128,1536]{1,0:T(8,128)(2,1)}, u32[]{:S(2)}) copy-start(bf16[128,1536]{1,0:T(8,128)(2,1)} %param.7) | copy-start | bytes 1179652
  43.9 60.0 %all-to-all-start = ((bf16[8,96,1536]{2,1,0:T(8,128)(2,1)}), bf16[8,96,1536]{2,1,0:T(8,128)(2,1)}, u32[]{:S(2)}, u32[]{:S(2)}) async-start(bf16[8,96,1536]{2,1,0:T(8,128)(2,1)} %bitcast.4), calls=%async_computation | async-start | bytes 4718592 | tf_op jit(solution)/shard_map/all_to_all | solution.py:63
  49.6 2.3 copy-start.4
  103.9 58.2 %all-to-all-start.1 = ((bf16[8,96,1536]{2,1,0:T(8,128)(2,1)}), bf16[8,96,1536]{2,1,0:T(8,128)(2,1)S(1)}, u32[]{:S(2)}, u32[]{:S(2)}) async-start(bf16[8,96,1536]{2,1,0:T(8,128)(2,1)} %bitcast.6), calls=%async_computation.1 | async-start | bytes 4718592 | tf_op jit(solution)/shard_map/all_to_all | solution.py:66
  107.5 40.4 %all-gather.2.cloned.1.call-start = ((), (), s32[]{:S(2)}) async-start(), calls=%async_computation.5 | async-start | bytes 2949120 | tf_op jit(solution)/shard_map/all_gather | solution.py:61
  162.1 1.5 copy-start
  232.3 51.4 %all-to-all-start.3 = ((bf16[4,2,147456]{2,1,0:T(2,128)(2,1)}), bf16[4,2,147456]{2,1,0:T(2,128)(2,1)S(1)}, u32[]{:S(2)}, u32[]{:S(2)}) async-start(bf16[4,2,147456]{2,1,0:T(2,128)(2,1)} %reshape.136), calls=%async_computation.3 | async-start | bytes 4718592 | tf_op jit(solution)/shard_map/all_to_all | solution.py:27
  283.7 32.2 %all-to-all-start.4 = ((bf16[4,2,147456]{2,1,0:T(2,128)(2,1)}), bf16[4,2,147456]{2,1,0:T(2,128)(2,1)}, u32[]{:S(2)}, u32[]{:S(2)}) async-start(bf16[4,2,147456]{2,1,0:T(2,128)(2,1)} %reshape.138), calls=%async_computation.4 | async-start | bytes 4718592 | tf_op jit(solution)/shard_map/all_to_all | solution.py:36
Sparse Core Ops, SparseCore 0:
  110.2 37.7 all-gather.1
